TPU v7x, 32 devices: a whole 2x2x4 slice. The times are simulated.
32 devices in a mesh: row: 4 (over y, core), col: 8 (over z, x).
Axes of the slice: x: 2, y: 2, z: 4, core: 2. Of those that a mesh axis runs over, the one named last changes fastest.
Arguments:
- strong_amp: float32 [512, 128, 128], P(('row', 'col')), may hold values from -3 to 3
- strong_rhs: float32 [512, 128, 128], P(('row', 'col')), may hold values from -6 to 6
- strong_left: bfloat16 [512, 128, 128], P(('row', 'col')), may hold values from -0.5 to 0.5
- strong_right: bfloat16 [512, 128, 128], P(('row', 'col')), may hold values from -0.5 to 0.5
- strong_energy: float32 [512, 128], P(('row', 'col')), may hold values from 1 to 4
- strong_intersection: bfloat16 [512, 16, 128, 128], P(('row', 'col')), may hold values from -0.375 to 0.375
- strong_nb: int32 [512, 16], P(('row', 'col')), may hold values from 0 to 39
- strong_live: int32 [512], P(('row', 'col')), may hold values from 1 to 16
- col_send: int32 [256, 2], P(('row', 'col')), may hold values from 0 to 15
- row_send: int32 [128, 2], P(('row', 'col')), may hold values from 0 to 15
- weak_amp: float32 [1024, 64, 64], P(('row', 'col')), may hold values from -3 to 3
- weak_rhs: float32 [1024, 64, 64], P(('row', 'col')), may hold values from -6 to 6
- weak_blocks: bfloat16 [1024, 64, 128], P(('row', 'col')), may hold values from -0.75 to 0.75
- weak_energy: float32 [1024, 64], P(('row', 'col')), may hold values from 1 to 4
- weak_intersection: bfloat16 [1024, 16, 64, 128], P(('row', 'col')), may hold values from -0.375 to 0.375
- weak_nb: int32 [1024, 16], P(('row', 'col')), may hold values from 0 to 39
Outputs:
- strong_next: float32 [512, 128, 128], P(('row', 'col'))
- weak_next: float32 [1024, 64, 64], P(('row', 'col'))
Inputs may be any that keep to these rules, and one draw needn't show every extreme that they name: `col_send`: entries name local strong pairs of the sending device. `row_send`: entries name local strong pairs of the sending device. `strong_nb`: entries index the reading device's pool. `weak_nb`: entries index the reading device's pool. The first strong_live neighbours of a pair are in use.
All inputs are finite; a program needn't handle non-finite values.
Results may differ from a plain program's by a relative error of at most 0.0024.
Values may be sent and summed in bfloat16 or wider, within the bound.
No kernel may reach another device: no remote copies, remote signals or barrier semaphores. Data moves between devices by JAX's collectives and lax.ppermute only.
A program may use at most 128 MiB of HBM per device.

v0:
```python
import jax
import jax.numpy as jnp
from jax import lax
from jax.sharding import PartitionSpec as P

UPDATES = 2


def sandwich(intersection, gathered, live_mask):
    half_way = (
        jnp.einsum(
            "snab,snbc->snac", intersection, gathered, preferred_element_type=jnp.float32
        ).astype(jnp.bfloat16)
        * live_mask
    )
    return jnp.einsum("snac,sndc->sad", half_way, intersection, preferred_element_type=jnp.float32)


def pair_terms(intersection, gathered, live_mask):
    return sandwich(intersection, gathered, live_mask)


def advance(amplitude, tiles_now, rhs, left, right, energy, coupling):
    inter = jnp.einsum("sab,sbc->sac", left, tiles_now, preferred_element_type=jnp.float32)
    inter = inter + jnp.einsum("sab,sbc->sac", tiles_now, right, preferred_element_type=jnp.float32)
    residual = rhs + inter + coupling
    return amplitude - residual / (energy[:, :, None] + energy[:, None, :])


def on_device(
    strong_amp,
    strong_rhs,
    strong_left,
    strong_right,
    strong_energy,
    strong_intersection,
    strong_nb,
    strong_live,
    col_send,
    row_send,
    weak_amp,
    weak_rhs,
    weak_blocks,
    weak_energy,
    weak_intersection,
    weak_nb,
):
    width = strong_amp.shape[1]
    live_mask = (
        jnp.arange(strong_nb.shape[1], dtype=jnp.int32)[None, :] < strong_live[:, None]
    ).astype(jnp.bfloat16)[:, :, None, None]
    weak_mask = jnp.ones((weak_nb.shape[0], weak_nb.shape[1], 1, 1), jnp.bfloat16)
    weak_width = weak_amp.shape[1]
    left_weak = weak_blocks[:, :, :weak_width]
    right_weak = weak_blocks[:, :, weak_width:]
    for update_step in range(UPDATES):
        tiles_now = strong_amp.astype(jnp.bfloat16)
        col_pool = lax.all_to_all(
            tiles_now[col_send], "col", split_axis=0, concat_axis=0, tiled=True
        )
        row_pool = lax.all_to_all(
            tiles_now[row_send], "row", split_axis=0, concat_axis=0, tiled=True
        )
        tile_pool = jnp.concatenate(
            [tiles_now, col_pool.reshape(-1, width, width), row_pool.reshape(-1, width, width)],
            axis=0,
        )
        coupling = pair_terms(strong_intersection, tile_pool[strong_nb], live_mask)
        weak_coupling = pair_terms(weak_intersection, tile_pool[weak_nb], weak_mask)
        weak_tiles = weak_amp.astype(jnp.bfloat16)
        strong_amp = advance(
            strong_amp, tiles_now, strong_rhs, strong_left, strong_right, strong_energy, coupling
        )
        weak_amp = advance(
            weak_amp, weak_tiles, weak_rhs, left_weak, right_weak, weak_energy, weak_coupling
        )
    return (strong_amp, weak_amp)


def solution(mesh):
    in_specs = (
        P(("row", "col"), None, None),
        P(("row", "col"), None, None),
        P(("row", "col"), None, None),
        P(("row", "col"), None, None),
        P(("row", "col"), None),
        P(("row", "col"), None, None, None),
        P(("row", "col"), None),
        P(("row", "col")),
        P(("row", "col"), None),
        P(("row", "col"), None),
        P(("row", "col"), None, None),
        P(("row", "col"), None, None),
        P(("row", "col"), None, None),
        P(("row", "col"), None),
        P(("row", "col"), None, None, None),
        P(("row", "col"), None),
    )
    out_specs = (P(("row", "col"), None, None), P(("row", "col"), None, None))
    return jax.shard_map(
        on_device, mesh=mesh, in_specs=in_specs, out_specs=out_specs, check_vma=False
    )
```

profile of v0, /device:TPU:0, one launch (start us, length us, event | category | flops | bytes accessed | tf_op | source)
XLA Modules:
  0.0 177.0 jit_solution(17885366510532251864)
XLA Ops:
  0.6 0.0 copy-start
  0.6 1.4 convert_element_type.39
  2.0 0.7 compare_select_fusion.2
  2.7 0.1 copy.25
  2.8 0.1 reshape.56
  2.9 1.3 gather_fusion.1
  4.2 4.3 %all-to-all-start.1 = ((bf16[4,2,128,128]{3,2,1,0:T(8,128)(2,1)}), bf16[4,2,128,128]{3,2,1,0:T(8,128)(2,1)S(1)}, u32[]{:S(2)}, u32[]{:S(2)}) async-start(bf16[4,2,128,128]{3,2,1,0:T(8,128)(2,1)} %bitcast.2), calls=%async_computation.1 | async-start | bytes 524288 | tf_op jit(solution)/shard_map/all_to_all | solution.py:61
  8.4 0.7 compare_select_fusion.3
  9.1 0.1 copy.24
  9.2 0.1 reshape.48
  9.3 1.4 gather_fusion
  10.7 0.7 compare_select_fusion.1
  11.4 0.1 reshape.64
  11.5 0.7 compare_select_fusion
  12.2 2.3 %all-to-all-done.1 = bf16[4,2,128,128]{3,2,1,0:T(8,128)(2,1)S(1)} async-done(((bf16[4,2,128,128]{3,2,1,0:T(8,128)(2,1)}), bf16[4,2,128,128]{3,2,1,0:T(8,128)(2,1)S(1)}, u32[]{:S(2)}, u32[]{:S(2)}) %all-to-all-start.1) | async-done | bytes 262176 | tf_op jit(solution)/shard_map/all_to_all | solution.py:61
  14.5 6.4 %all-to-all-start = ((bf16[8,2,128,128]{3,2,1,0:T(8,128)(2,1)}), bf16[8,2,128,128]{3,2,1,0:T(8,128)(2,1)S(1)}, u32[]{:S(2)}, u32[]{:S(2)}) async-start(bf16[8,2,128,128]{3,2,1,0:T(8,128)(2,1)} %bitcast), calls=%async_computation | async-start | bytes 1048576 | tf_op jit(solution)/shard_map/all_to_all | solution.py:58
  20.9 0.1 copy.28
  20.9 0.1 reshape.96
  21.0 0.7 fusion.60
  21.8 2.7 %fusion.63 = f32[16,128,128]{2,1,0:T(8,128)} fusion(bf16[16,128,128]{2,1,0:T(8,128)(2,1)} %param.18, f32[16,128,128]{2,1,0:T(8,128)} %param.16), kind=kOutput, calls=%fused_computation.78 | convolution fusion | flops 67371008 | bytes 2621440 | tf_op jit(solution)/shard_map/sab,sbc->sac/dot_general | solution.py:24
  24.4 2.7 %fusion.54 = f32[32,64,64]{2,1,0:T(8,128)} fusion(bf16[32,64,128]{2,1,0:T(8,128)(2,1)} %param.28, f32[32,64,64]{2,1,0:T(8,128)} %param.26), kind=kOutput, calls=%fused_computation.60 | convolution fusion | flops 16908288 | bytes 1572864 | tf_op jit(solution)/shard_map/sab,sbc->sac/dot_general | solution.py:24
  27.1 8.0 %all-to-all-done = bf16[8,2,128,128]{3,2,1,0:T(8,128)(2,1)S(1)} async-done(((bf16[8,2,128,128]{3,2,1,0:T(8,128)(2,1)}), bf16[8,2,128,128]{3,2,1,0:T(8,128)(2,1)S(1)}, u32[]{:S(2)}, u32[]{:S(2)}) %all-to-all-start) | async-done | bytes 524320 | tf_op jit(solution)/shard_map/all_to_all | solution.py:58
  35.1 0.2 pad_maximum_fusion
  35.2 8.6 %gather_fusion.2 = bf16[256,128,128]{2,1,0:T(8,128)(2,1)} fusion(bf16[40,128,128]{2,1,0:T(8,128)(2,1)S(1)} %pad_maximum_fusion, s32[1024]{0:T(1024)S(1)} %pad_clamp_fusion.1), kind=kCustom, calls=%fused_computation.2 | custom fusion | bytes 16778240 | tf_op jit(solution)/shard_map/gather | solution.py:68
  43.9 11.7 %fusion.24 = f32[16,128,128]{2,1,0:T(8,128)} fusion(bf16[16,16,128,128]{3,2,1,0:T(8,128)(2,1)} %param.21, bf16[16,16,128,128]{3,2,1,0:T(8,128)(2,1)} %bitcast.89, bf16[16,16]{1,0:T(8,128)(2,1)S(1)} %fusion.60), kind=kOutput, calls=%fused_computation.32 | convolution fusion | flops 2155872256 | bytes 17826304 | tf_op jit(solution)/shard_map/snac,sndc->sad/dot_general | solution.py:16
  55.6 0.0 copy-done
  55.6 0.0 copy-done.2
  55.6 3.3 %fusion.61 = (bf16[16,128,128]{2,1,0:T(8,128)(2,1)S(1)}, f32[16,128,128]{2,1,0:T(8,128)}) fusion(f32[16,128,128]{2,1,0:T(8,128)S(1)} %copy-done.2, f32[16,128]{1,0:T(8,128)S(1)} %copy-done.9, f32[16,128,128]{2,1,0:T(8,128)} %fusion.24, f32[16,128,128]{2,1,0:T(8,128)} %param.17, f32[16,128,128]{2,1,0:T(8,128)} %fusion.63, bf16[16,128,128]{2,1,0:T(8,128)(2,1)S(1)} %copy-done), kind=kOutput, calls=%fused_computation.76 | convolution fusion | flops 69206016 | bytes 6299648 | tf_op jit(solution)/shard_map/sab,sbc->sac/dot_general | solution.py:25
  58.9 1.3 gather_fusion.4
  60.2 3.6 %all-to-all-start.3 = ((bf16[4,2,128,128]{3,2,1,0:T(8,128)(2,1)}), bf16[4,2,128,128]{3,2,1,0:T(8,128)(2,1)S(1)}, u32[]{:S(2)}, u32[]{:S(2)}) async-start(bf16[4,2,128,128]{3,2,1,0:T(8,128)(2,1)} %bitcast.11), calls=%async_computation.3 | async-start | bytes 524288 | tf_op jit(solution)/shard_map/all_to_all | solution.py:61
  63.8 13.9 %gather_fusion.6 = bf16[512,128,128]{2,1,0:T(8,128)(2,1)} fusion(bf16[40,128,128]{2,1,0:T(8,128)(2,1)S(1)} %pad_maximum_fusion, s32[1024]{0:T(1024)S(1)} %pad_clamp_fusion), kind=kCustom, calls=%fused_computation.6 | custom fusion | bytes 33556480 | tf_op jit(solution)/shard_map/gather | solution.py:69
  77.7 18.1 %fusion.30 = f32[32,64,64]{2,1,0:T(8,128)} fusion(bf16[32,16,64,128]{3,2,1,0:T(8,128)(2,1)} %param.30, bf16[32,16,128,128]{3,2,1,0:T(8,128)(2,1)} %bitcast.87), kind=kOutput, calls=%fused_computation.34 | convolution fusion | flops 1614807040 | bytes 25690112 | tf_op jit(solution)/shard_map/snac,sndc->sad/dot_general | solution.py:16
  95.8 1.4 gather_fusion.3
  97.2 0.0 all-to-all-done.3
  97.2 3.7 %all-to-all-start.2 = ((bf16[8,2,128,128]{3,2,1,0:T(8,128)(2,1)}), bf16[8,2,128,128]{3,2,1,0:T(8,128)(2,1)S(1)}, u32[]{:S(2)}, u32[]{:S(2)}) async-start(bf16[8,2,128,128]{3,2,1,0:T(8,128)(2,1)} %bitcast.9), calls=%async_computation.2 | async-start | bytes 1048576 | tf_op jit(solution)/shard_map/all_to_all | solution.py:58
  100.9 1.3 fusion.65
  102.3 3.0 %fusion.46 = f32[32,64,64]{2,1,0:T(8,128)S(1)} fusion(f32[32,64,64]{2,1,0:T(8,128)} %param.26, f32[32,64,64]{2,1,0:T(8,128)} %fusion.30, f32[32,64,64]{2,1,0:T(8,128)} %param.27, f32[32,64,64]{2,1,0:T(8,128)} %fusion.54, f32[32,64]{1,0:T(8,128)S(1)} %copy-done.8, bf16[32,64,128]{2,1,0:T(8,128)(2,1)S(1)} %copy-done.3), kind=kOutput, calls=%fused_computation.49 | convolution fusion | flops 17694720 | bytes 6324224 | tf_op jit(solution)/shard_map/sab,sbc->sac/dot_general | solution.py:25
  105.3 1.4 fusion.50
  106.7 9.1 %all-to-all-done.2 = bf16[8,2,128,128]{3,2,1,0:T(8,128)(2,1)S(1)} async-done(((bf16[8,2,128,128]{3,2,1,0:T(8,128)(2,1)}), bf16[8,2,128,128]{3,2,1,0:T(8,128)(2,1)S(1)}, u32[]{:S(2)}, u32[]{:S(2)}) %all-to-all-start.2) | async-done | bytes 524320 | tf_op jit(solution)/shard_map/all_to_all | solution.py:58
  115.8 0.8 copy-done.6
  116.6 1.3 pad_maximum_fusion.1
  117.9 8.6 %gather_fusion.5 = bf16[256,128,128]{2,1,0:T(8,128)(2,1)} fusion(bf16[40,128,128]{2,1,0:T(8,128)(2,1)S(1)} %pad_maximum_fusion.1, s32[1024]{0:T(1024)S(1)} %pad_clamp_fusion.1), kind=kCustom, calls=%fused_computation.5 | custom fusion | bytes 16778240 | tf_op jit(solution)/shard_map/gather | solution.py:68
  126.5 13.9 %gather_fusion.7 = bf16[512,128,128]{2,1,0:T(8,128)(2,1)} fusion(bf16[40,128,128]{2,1,0:T(8,128)(2,1)S(1)} %pad_maximum_fusion.1, s32[1024]{0:T(1024)S(1)} %pad_clamp_fusion), kind=kCustom, calls=%fused_computation.7 | custom fusion | bytes 33556480 | tf_op jit(solution)/shard_map/gather | solution.py:69
  140.5 11.7 %fusion.27 = f32[16,128,128]{2,1,0:T(8,128)} fusion(bf16[16,16,128,128]{3,2,1,0:T(8,128)(2,1)} %param.21, bf16[16,16,128,128]{3,2,1,0:T(8,128)(2,1)} %bitcast.88, bf16[16,16]{1,0:T(8,128)(2,1)S(1)} %fusion.60), kind=kOutput, calls=%fused_computation.33 | convolution fusion | flops 2155872256 | bytes 17826304 | tf_op jit(solution)/shard_map/snac,sndc->sad/dot_general | solution.py:16
  152.1 18.1 %fusion.33 = f32[32,64,64]{2,1,0:T(8,128)} fusion(bf16[32,16,64,128]{3,2,1,0:T(8,128)(2,1)} %param.30, bf16[32,16,128,128]{3,2,1,0:T(8,128)(2,1)} %bitcast.86), kind=kOutput, calls=%fused_computation.35 | convolution fusion | flops 1614807040 | bytes 25690112 | tf_op jit(solution)/shard_map/snac,sndc->sad/dot_general | solution.py:16
  170.2 0.0 copy-done.4
  170.2 3.3 %fusion.39 = f32[32,64,64]{2,1,0:T(8,128)} fusion(f32[32,64,64]{2,1,0:T(8,128)S(1)} %fusion.46, f32[32,64,64]{2,1,0:T(8,128)} %fusion.33, f32[32,64,64]{2,1,0:T(8,128)} %param.27, f32[32,64,64]{2,1,0:T(8,128)} %fusion.50, f32[32,64]{1,0:T(8,128)S(1)} %copy-done.8, bf16[32,64,128]{2,1,0:T(8,128)(2,1)S(1)} %copy-done.4), kind=kOutput, calls=%fused_computation.40 | convolution fusion | flops 17694720 | bytes 4751360 | tf_op jit(solution)/shard_map/sab,sbc->sac/dot_general | solution.py:24
  173.5 3.6 %fusion.43 = f32[16,128,128]{2,1,0:T(8,128)} fusion(f32[16,128,128]{2,1,0:T(8,128)} %get-tuple-element.3, f32[16,128,128]{2,1,0:T(8,128)} %fusion.27, f32[16,128,128]{2,1,0:T(8,128)} %param.17, f32[16,128,128]{2,1,0:T(8,128)} %fusion.65, bf16[16,128,128]{2,1,0:T(8,128)(2,1)S(1)} %copy-done.5, bf16[16,128,128]{2,1,0:T(8,128)(2,1)S(1)} %get-tuple-element.2, ...), kind=kOutput, calls=%fused_computation.45 | convolution fusion | flops 68681728 | bytes 6299648 | tf_op jit(solution)/shard_map/sab,sbc->sac/dot_general | solution.py:24
  (19 shorter events, 0.1 us)
Async XLA Ops:
  0.6 55.0 %copy-start = (bf16[16,128,128]{2,1,0:T(8,128)(2,1)S(1)}, bf16[16,128,128]{2,1,0:T(8,128)(2,1)}, u32[]{:S(2)}) copy-start(bf16[16,128,128]{2,1,0:T(8,128)(2,1)} %param.19) | copy-start | bytes 1572868
  4.2 10.3 %all-to-all-start.1 = ((bf16[4,2,128,128]{3,2,1,0:T(8,128)(2,1)}), bf16[4,2,128,128]{3,2,1,0:T(8,128)(2,1)S(1)}, u32[]{:S(2)}, u32[]{:S(2)}) async-start(bf16[4,2,128,128]{3,2,1,0:T(8,128)(2,1)} %bitcast.2), calls=%async_computation.1 | async-start | bytes 524288 | tf_op jit(solution)/shard_map/all_to_all | solution.py:61
  14.5 20.6 %all-to-all-start = ((bf16[8,2,128,128]{3,2,1,0:T(8,128)(2,1)}), bf16[8,2,128,128]{3,2,1,0:T(8,128)(2,1)S(1)}, u32[]{:S(2)}, u32[]{:S(2)}) async-start(bf16[8,2,128,128]{3,2,1,0:T(8,128)(2,1)} %bitcast), calls=%async_computation | async-start | bytes 1048576 | tf_op jit(solution)/shard_map/all_to_all | solution.py:58
  43.9 11.7 %copy-start.2 = (f32[16,128,128]{2,1,0:T(8,128)S(1)}, f32[16,128,128]{2,1,0:T(8,128)}, u32[]{:S(2)}) copy-start(f32[16,128,128]{2,1,0:T(8,128)} %param.16) | copy-start | bytes 3145732
  43.9 11.7 %copy-start.9 = (f32[16,128]{1,0:T(8,128)S(1)}, f32[16,128]{1,0:T(8,128)}, u32[]{:S(2)}) copy-start(f32[16,128]{1,0:T(8,128)} %param.20) | copy-start | bytes 24580
  60.2 37.0 %all-to-all-start.3 = ((bf16[4,2,128,128]{3,2,1,0:T(8,128)(2,1)}), bf16[4,2,128,128]{3,2,1,0:T(8,128)(2,1)S(1)}, u32[]{:S(2)}, u32[]{:S(2)}) async-start(bf16[4,2,128,128]{3,2,1,0:T(8,128)(2,1)} %bitcast.11), calls=%async_computation.3 | async-start | bytes 524288 | tf_op jit(solution)/shard_map/all_to_all | solution.py:61
  77.7 24.6 %copy-start.3 = (bf16[32,64,128]{2,1,0:T(8,128)(2,1)S(1)}, bf16[32,64,128]{2,1,0:T(8,128)(2,1)}, u32[]{:S(2)}) copy-start(bf16[32,64,128]{2,1,0:T(8,128)(2,1)} %param.28) | copy-start | bytes 1572868
  77.7 24.6 %copy-start.8 = (f32[32,64]{1,0:T(8,128)S(1)}, f32[32,64]{1,0:T(8,128)}, u32[]{:S(2)}) copy-start(f32[32,64]{1,0:T(8,128)} %param.29) | copy-start | bytes 24580
  97.2 18.6 %copy-start.7 = (bf16[4,2,128,128]{3,2,1,0:T(8,128)(2,1)}, bf16[4,2,128,128]{3,2,1,0:T(8,128)(2,1)S(1)}, u32[]{:S(2)}) copy-start(bf16[4,2,128,128]{3,2,1,0:T(8,128)(2,1)S(1)} %all-to-all-done.3) | copy-start | bytes 786436
  97.2 18.6 %all-to-all-start.2 = ((bf16[8,2,128,128]{3,2,1,0:T(8,128)(2,1)}), bf16[8,2,128,128]{3,2,1,0:T(8,128)(2,1)S(1)}, u32[]{:S(2)}, u32[]{:S(2)}) async-start(bf16[8,2,128,128]{3,2,1,0:T(8,128)(2,1)} %bitcast.9), calls=%async_computation.2 | async-start | bytes 1048576 | tf_op jit(solution)/shard_map/all_to_all | solution.py:58
  115.8 0.8 copy-start.6
  152.1 18.1 %copy-start.4 = (bf16[32,64,128]{2,1,0:T(8,128)(2,1)S(1)}, bf16[32,64,128]{2,1,0:T(8,128)(2,1)}, u32[]{:S(2)}) copy-start(bf16[32,64,128]{2,1,0:T(8,128)(2,1)} %param.28) | copy-start | bytes 1572868
  152.1 21.4 %copy-start.5 = (bf16[16,128,128]{2,1,0:T(8,128)(2,1)S(1)}, bf16[16,128,128]{2,1,0:T(8,128)(2,1)}, u32[]{:S(2)}) copy-start(bf16[16,128,128]{2,1,0:T(8,128)(2,1)} %param.18) | copy-start | bytes 1572868
  152.1 24.9 %copy-start.1 = (bf16[16,128,128]{2,1,0:T(8,128)(2,1)S(1)}, bf16[16,128,128]{2,1,0:T(8,128)(2,1)}, u32[]{:S(2)}) copy-start(bf16[16,128,128]{2,1,0:T(8,128)(2,1)} %param.19) | copy-start | bytes 1572868
where the time goes:
time: 178 us; the launch traced here: 177 us
  matrix products  80.7 us (45%)
  local copies, waits for them, and re-layouts  51.9 us (29%)
  waiting for transfers between devices  19.4 us (11%)
  starting transfers between devices  18 us (10%)
  other arithmetic  6.33 us (4%)
    dot_general x4, matrix products, sandwich(): jnp.einsum('snac,sndc->sad', half_way, intersection, preferred_element_ty...  59.6 us
    gather x2, local copies, waits for them, and re-layouts, on_device(): weak_coupling = pair_terms(weak_intersection, tile_pool[weak_nb], weak_mask)  27.8 us
    gather x2, local copies, waits for them, and re-layouts, on_device(): coupling = pair_terms(strong_intersection, tile_pool[strong_nb], live_mask)  17.2 us
    all_to_all x2, waiting for transfers between devices, on_device(): lax.all_to_all(tiles_now[col_send], 'col', split_axis=0, concat_axis=0, t...  17.2 us
    dot_general x4, matrix products, advance(): jnp.einsum('sab,sbc->sac', left, tiles_now, preferred_element_type=jnp.fl...  12.1 us
    all_to_all x2, starting transfers between devices, on_device(): lax.all_to_all(tiles_now[col_send], 'col', split_axis=0, concat_axis=0, t...  10.1 us
    dot_general x4, matrix products, advance(): jnp.einsum('sab,sbc->sac', tiles_now, right, preferred_element_type=jnp.f...  9.05 us
    all_to_all x2, starting transfers between devices, on_device(): lax.all_to_all(tiles_now[row_send], 'row', split_axis=0, concat_axis=0, t...  7.85 us
  transfers between devices with their start and end apart: 4, of which 3 were waited for; matrix products, arithmetic and copies ran while one was open for 28% of the time, Pallas kernels for 0%

commit v1 on v0

v1 whole, which is shorter than its diff:
```python
import functools

import jax
import jax.numpy as jnp
from jax import lax
from jax.experimental import pallas as pl
from jax.experimental.pallas import tpu as pltpu
from jax.sharding import PartitionSpec as P

F32 = jnp.float32
BF16 = jnp.bfloat16
MIB = 1 << 20
GROUP = 4
STRONG_ITEMS = 4
WEAK_ITEMS = 8
SHIFT = 8


VM = pl.BlockSpec(memory_space=pltpu.VMEM)
SM = pl.BlockSpec(memory_space=pltpu.SMEM)
HB = pl.BlockSpec(memory_space=pltpu.HBM)
ANY = pl.BlockSpec(memory_space=pl.ANY)


def call(body, outs, in_specs, flops, nbytes, scratch):
    return pl.pallas_call(
        body,
        out_shape=[jax.ShapeDtypeStruct(s, d) for s, d in outs],
        in_specs=in_specs,
        out_specs=[HB for _ in outs],
        scratch_shapes=list(scratch),
        cost_estimate=pl.CostEstimate(
            flops=int(flops), bytes_accessed=int(nbytes), transcendentals=0
        ),
        compiler_params=pltpu.CompilerParams(vmem_limit_bytes=60 * 1024 * 1024),
    )


class Copies:
    def __init__(self, sems):
        self.sems, self.used, self.named = sems, 0, {}

    def start(self, name, src, dst):
        copy = pltpu.make_async_copy(src, dst, self.sems.at[self.used])
        self.used += 1
        self.named.setdefault(name, []).append(copy)
        copy.start()

    def wait(self, *names):
        for name in names:
            for copy in self.named.pop(name):
                copy.wait()


def dot(a, b):
    return jnp.dot(a, b, preferred_element_type=F32)


def dot_t(a, b):
    return lax.dot_general(a, b, (((1,), (1,)), ((), ())), preferred_element_type=F32)


def partner(i, k, n):
    return i ^ k if n & (n - 1) == 0 else lax.rem(i + k, n)


def origin(i, k, n):
    return i ^ k if n & (n - 1) == 0 else lax.rem(i + n - k, n)


def perm(k, n):
    if n & (n - 1) == 0:
        return [(s, s ^ k) for s in range(n)]
    return [(s, (s + k) % n) for s in range(n)]


def each(n, f, unroll=1):
    if n % unroll:
        unroll = 1

    def body(i, c):
        for u in range(unroll):
            f(i * unroll + u)
        return c

    lax.fori_loop(0, n // unroll, body, 0)


def start_sends(copies, me, tiles, col_send, row_send, col_out, row_out):
    cap = col_out.shape[1]
    for d in range(col_out.shape[0]):
        for s in range(cap):
            copies.start("sent", tiles.at[col_send[d, s]], col_out.at[d, s])
    n = len(row_out) + 1
    for k in range(1, n):
        d = partner(me[0], k, n)
        for s in range(cap):
            copies.start("sent", tiles.at[row_send[d, s]], row_out[k - 1].at[s])


def prep_kernel(me, col_send_h, row_send_h, amp_h, tiles_out, col_out, *rest):
    *row_out, amp, tiles, col_send, row_send, sems = rest
    copies = Copies(sems)
    parts = 4
    step = amp.shape[0] // parts
    copies.start("lists", col_send_h, col_send)
    copies.start("lists", row_send_h, row_send)
    for i in range(parts):
        at = pl.ds(i * step, step)
        copies.start(i, amp_h.at[at], amp.at[at])
    for i in range(parts):
        copies.wait(i)
        for j in range(step):
            tiles[i * step + j] = amp[i * step + j].astype(BF16)
    copies.wait("lists")
    start_sends(copies, me, tiles, col_send, row_send, col_out, row_out)
    copies.start("sent", tiles, tiles_out)
    copies.wait("sent")


def weak_inter(blocks, t):
    q = t.shape[0]
    return dot(blocks[:, :q], t) + dot(t, blocks[:, q:])


def strong_inter(left, right, t):
    return dot(left, t) + dot(t, right)


def inverse(e):
    n = e.shape[1]
    rows = jnp.broadcast_to(e, (n, n))
    return 1.0 / (rows.T + rows)


def start_near(copies, me, tiles, col_send, row_send, pool, nc):
    own = tiles.shape[0]
    cap = col_send.shape[1]
    copies.start("near", tiles, pool.at[pl.ds(0, own)])
    for s in range(cap):
        copies.start("near", tiles.at[col_send[me[1], s]], pool.at[own + me[1] * cap + s])
        copies.start(
            "near", tiles.at[row_send[me[0], s]], pool.at[own + (nc + me[0]) * cap + s]
        )


def start_pool(copies, me, tiles, row_send, pool, got, row_got):
    own = tiles.shape[0]
    nc, cap = got.shape[:2]
    copies.start("near", tiles, pool.at[pl.ds(0, own)])
    for c in range(nc):
        copies.start("near", got.at[c], pool.at[pl.ds(own + c * cap, cap)])
    at = own + nc * cap
    n = len(row_got) + 1
    for s in range(cap):
        copies.start("near", tiles.at[row_send[me[0], s]], pool.at[at + me[0] * cap + s])
    for k in range(1, n):
        o = origin(me[0], k, n)
        copies.start("near", row_got[k - 1], pool.at[pl.ds(at + o * cap, cap)])


class Rows:
    def __init__(self, src, dst, sems):
        self.src, self.dst, self.sems = src, dst, sems
        self.n = dst.shape[0]

    def copy(self, i):
        return pltpu.make_async_copy(self.src.at[i], self.dst.at[i], self.sems.at[i])

    def start(self):
        for i in range(self.n):
            self.copy(i).start()

    def wait(self, ready, upto):
        def one(i, c):
            self.copy(i).wait()
            return c

        lax.fori_loop(ready, upto, one, 0)
        return jnp.maximum(ready, upto)


def make_list(items, n, near, total, phase, step):
    most = GROUP

    def one(p, at):
        full = near[p] >> 2
        if phase == 0:
            first, count = 0, full
        else:
            first, count = full, total(p) - full
        for j in range(most):
            items[at + j] = p * most + first + j
        return at + count

    count = lax.fori_loop(0, n, one, 0)
    for j in range(step):
        items[count + j] = n * most
    return (count + step - 1) // step


def run_items(items, steps, step, pool, order, inter, rows, acc, live):
    n = inter.shape[0]

    def body(i, ready):
        last = jnp.minimum(items[i * step + step - 1] >> 2, n - 1)
        ready = rows.wait(ready, last + 1)
        for u in range(step):
            item = items[i * step + u]
            at = item >> 2
            p = jnp.minimum(at, n - 1)
            j = (item & 3) * GROUP
            mids, weights = [], []
            for g in range(GROUP):
                e = order[p, j + g]
                w = inter[p, e >> SHIFT]
                m = dot(w, pool[e & ((1 << SHIFT) - 1)]).astype(BF16)
                if live is not None:
                    m = jnp.where(j + g < live[p], m, jnp.zeros_like(m))
                mids.append(m)
                weights.append(w)
            acc[at] += dot_t(jnp.concatenate(mids, axis=1), jnp.concatenate(weights, axis=1))
        return ready

    ready = lax.fori_loop(0, steps, body, jnp.int32(0))
    rows.wait(ready, n)


def run_strong(phase, items, pool, order, near, live, inter, rows, acc):
    n = inter.shape[0]
    steps = make_list(items, n, near, lambda p: (live[p] + 3) >> 2, phase, STRONG_ITEMS)
    run_items(items, steps, STRONG_ITEMS, pool, order, inter, rows, acc, live)


def run_weak(phase, items, pool, order, near, inter, rows, acc):
    n, count = inter.shape[:2]
    steps = make_list(items, n, near, lambda p: count >> 2, phase, WEAK_ITEMS)
    run_items(items, steps, WEAK_ITEMS, pool, order, inter, rows, acc, None)


def first_kernel(
    nc, me, s_order, s_near, live, w_order, w_near, col_send, row_send,
    tiles_h, s_rhs_h, s_left_h, s_right_h, s_energy_h, w_amp_h, w_rhs_h, w_blocks_h, w_energy_h,
    s_int_h, w_int_h,
    s_acc_out, w_acc_out, s_inv_out, w_inv_out,
    pool, s_rhs, s_left, s_right, s_energy, w_amp, w_rhs, w_blocks, w_energy, s_all, w_all,
    s_acc, w_acc, s_inv, w_inv, s_items, w_items, sems, s_sems, w_sems,
):
    copies = Copies(sems)
    start_near(copies, me, tiles_h, col_send, row_send, pool, nc)
    for src, dst in ((s_left_h, s_left), (s_right_h, s_right), (s_rhs_h, s_rhs), (s_energy_h, s_energy)):
        copies.start("s", src, dst)
    for src, dst in ((w_amp_h, w_amp), (w_blocks_h, w_blocks), (w_rhs_h, w_rhs), (w_energy_h, w_energy)):
        copies.start("w", src, dst)
    s_rows, w_rows = Rows(s_int_h, s_all, s_sems), Rows(w_int_h, w_all, w_sems)
    s_rows.start()
    w_rows.start()
    copies.wait("near", "s")

    def strong(p):
        s_acc[p] = s_rhs[p] + strong_inter(s_left[p], s_right[p], pool[p])
        s_inv[p] = inverse(s_energy[pl.ds(p, 1), :])

    each(s_rhs.shape[0], strong, 2)
    copies.wait("w")

    def weak(w):
        w_acc[w] = w_rhs[w] + weak_inter(w_blocks[w], w_amp[w].astype(BF16))
        w_inv[w] = inverse(w_energy[pl.ds(w, 1), :])

    each(w_amp.shape[0], weak, 2)
    copies.start("out", s_inv, s_inv_out)
    copies.start("out", w_inv, w_inv_out)
    run_strong(0, s_items, pool, s_order, s_near, live, s_all, s_rows, s_acc)
    copies.start("out", s_acc.at[pl.ds(0, s_inv.shape[0])], s_acc_out)
    run_weak(0, w_items, pool, w_order, w_near, w_all, w_rows, w_acc)
    copies.start("out", w_acc.at[pl.ds(0, w_inv.shape[0])], w_acc_out)
    copies.wait("out")


def strong_kernel(
    me, s_order, s_near, live, col_send, row_send, tiles_h, got, s_int_h, s_acc_h, s_inv_h, amp_h,
    *rest,
):
    n_row = (len(rest) - 12) // 2
    row_got, (amp_out, tiles_out, col_out), row_out = (
        rest[:n_row], rest[n_row : n_row + 3], rest[n_row + 3 : 2 * n_row + 3]
    )
    pool, s_all, s_acc, s_inv, amp, tiles, s_items, sems, s_sems = rest[2 * n_row + 3 :]
    n = amp.shape[0]
    copies = Copies(sems)
    start_pool(copies, me, tiles_h, row_send, pool, got, row_got)
    copies.start("acc", s_acc_h, s_acc.at[pl.ds(0, n)])
    rows = Rows(s_int_h, s_all, s_sems)
    rows.start()
    copies.start("end", amp_h, amp)
    copies.start("end", s_inv_h, s_inv)
    copies.wait("near", "acc")
    run_strong(1, s_items, pool, s_order, s_near, live, s_all, rows, s_acc)
    copies.wait("end")

    def finish(p):
        new = amp[p] - s_acc[p] * s_inv[p]
        amp[p] = new
        tiles[p] = new.astype(BF16)

    each(n, finish, 2)
    start_sends(copies, me, tiles, col_send, row_send, col_out, row_out)
    copies.start("sent", tiles, tiles_out)
    copies.start("sent", amp, amp_out)
    copies.wait("sent")


def middle_kernel(
    nc, me, s_order, s_near, live, w_order, w_near, col_send, row_send,
    tiles_h, got, tiles1_h, w_acc_h, w_inv_h, w_amp_h, w_rhs_h, w_blocks_h, s_rhs_h, s_left_h,
    s_right_h, s_int_h, w_int_h, *rest,
):
    n_row = len(rest) - 20
    row_got, (w_out, s_acc_out, w_acc_out) = rest[:n_row], rest[n_row : n_row + 3]
    (
        pool, pool1, w_acc, w_inv, w_amp, w_rhs, w_blocks, s_rhs, s_left, s_right, s_all, w_all,
        s_acc, s_items, w_items, sems, s_sems,
    ) = rest[n_row + 3 :]
    wp = w_amp.shape[0]
    w_sems = s_sems.at[1]
    copies = Copies(sems)
    start_pool(copies, me, tiles_h, row_send, pool, got, row_got)
    copies.start("acc", w_acc_h, w_acc.at[pl.ds(0, wp)])
    w_rows = Rows(w_int_h, w_all, w_sems)
    w_rows.start()
    for src, dst in ((w_inv_h, w_inv), (w_amp_h, w_amp), (w_rhs_h, w_rhs), (w_blocks_h, w_blocks)):
        copies.start("w", src, dst)
    copies.wait("near", "acc")
    start_near(copies, me, tiles1_h, col_send, row_send, pool1, nc)
    for src, dst in ((s_left_h, s_left), (s_right_h, s_right), (s_rhs_h, s_rhs)):
        copies.start("s", src, dst)
    s_rows = Rows(s_int_h, s_all, s_sems.at[0])
    s_rows.start()
    run_weak(1, w_items, pool, w_order, w_near, w_all, w_rows, w_acc)
    copies.wait("w")

    def weak(w):
        new = w_amp[w] - w_acc[w] * w_inv[w]
        w_amp[w] = new
        w_acc[w] = w_rhs[w] + weak_inter(w_blocks[w], new.astype(BF16))

    each(wp, weak, 4)
    copies.start("out", w_amp, w_out)
    copies.wait("near", "s")

    def strong(p):
        s_acc[p] = s_rhs[p] + strong_inter(s_left[p], s_right[p], pool1[p])

    each(s_rhs.shape[0], strong, 2)
    run_strong(0, s_items, pool1, s_order, s_near, live, s_all, s_rows, s_acc)
    copies.start("out", s_acc.at[pl.ds(0, s_rhs.shape[0])], s_acc_out)
    run_weak(0, w_items, pool1, w_order, w_near, w_all, NoRows(), w_acc)
    copies.start("out", w_acc.at[pl.ds(0, wp)], w_acc_out)
    copies.wait("out")


class NoRows:
    def wait(self, ready, upto):
        return ready


def last_kernel(
    me, s_order, s_near, live, w_order, w_near, row_send, tiles_h, got, s_int_h, w_int_h, s_acc_h,
    w_acc_h, s_inv_h, w_inv_h, s_amp_h, w_amp_h, *rest,
):
    n_row = len(rest) - 16
    row_got, (s_out, w_out) = rest[:n_row], rest[n_row : n_row + 2]
    (
        pool, s_all, w_all, s_acc, w_acc, s_inv, w_inv, s_amp, w_amp, s_items, w_items, sems,
        s_sems, w_sems,
    ) = rest[n_row + 2 :]
    n, wp = s_amp.shape[0], w_amp.shape[0]
    copies = Copies(sems)
    start_pool(copies, me, tiles_h, row_send, pool, got, row_got)
    copies.start("s", s_acc_h, s_acc.at[pl.ds(0, n)])
    s_rows, w_rows = Rows(s_int_h, s_all, s_sems), Rows(w_int_h, w_all, w_sems)
    s_rows.start()
    copies.start("s_end", s_amp_h, s_amp)
    copies.start("s_end", s_inv_h, s_inv)
    copies.start("w", w_acc_h, w_acc.at[pl.ds(0, wp)])
    w_rows.start()
    copies.start("w_end", w_amp_h, w_amp)
    copies.start("w_end", w_inv_h, w_inv)
    copies.wait("near", "s")
    run_strong(1, s_items, pool, s_order, s_near, live, s_all, s_rows, s_acc)
    copies.wait("s_end")

    def strong(p):
        s_amp[p] = s_amp[p] - s_acc[p] * s_inv[p]

    each(n, strong, 2)
    copies.start("out", s_amp, s_out)
    copies.wait("w")
    run_weak(1, w_items, pool, w_order, w_near, w_all, w_rows, w_acc)
    copies.wait("w_end")

    def weak(w):
        w_amp[w] = w_amp[w] - w_acc[w] * w_inv[w]

    each(wp, weak, 4)
    copies.start("out", w_amp, w_out)
    copies.wait("out")


def ordered(nb, far, live):
    count = nb.shape[1]
    place = jnp.arange(count, dtype=jnp.int32)
    used = place[None, :] < live[:, None]
    key = jnp.where(used, jnp.where(far, count, 0), 2 * count) + place[None, :]
    at = jnp.sum((key[:, None, :] < key[:, :, None]).astype(jnp.int32), axis=2)
    packed = (place[None, :] << SHIFT) + nb
    order = jnp.sum(jnp.where(at[:, :, None] == place[None, None, :], packed[:, :, None], 0), axis=1)
    near = jnp.sum((used & ~far).astype(jnp.int32), axis=1)
    return order, near


def on_device(
    nr, nc, strong_amp, strong_rhs, strong_left, strong_right, strong_energy, strong_intersection,
    strong_nb, strong_live, col_send, row_send, weak_amp, weak_rhs, weak_blocks, weak_energy,
    weak_intersection, weak_nb,
):
    sp, width = strong_amp.shape[:2]
    wp, q = weak_amp.shape[:2]
    count = strong_nb.shape[1]
    cap = col_send.shape[1]
    row, col = lax.axis_index("row"), lax.axis_index("col")
    me = jnp.stack([row, col]).astype(jnp.int32)
    s_shape, w_shape = (sp, width, width), (wp, q, q)
    s_f32, w_f32 = pltpu.VMEM(s_shape, F32), pltpu.VMEM(w_shape, F32)
    s_bf16, blocks = pltpu.VMEM(s_shape, BF16), pltpu.VMEM(weak_blocks.shape, BF16)
    s_sums = pltpu.VMEM((sp + 1, width, width), F32)
    w_sums = pltpu.VMEM((wp + 1, q, q), F32)
    s_all = pltpu.VMEM(strong_intersection.shape, BF16)
    w_all = pltpu.VMEM(weak_intersection.shape, BF16)
    pool = pltpu.VMEM((sp + cap * (nc + nr), width, width), BF16)
    row_shapes = [((cap, width, width), BF16)] * (nr - 1)
    col_shape = ((nc, cap, width, width), BF16)
    s_flops = 4 * sp * count * width**3
    w_flops = 2 * wp * count * (q * width * width + q * q * width)
    a_flops = 4 * sp * width**3
    s_bytes, w_bytes = strong_intersection.size * 2, weak_intersection.size * 2
    s_items = pltpu.SMEM((sp * count // GROUP + GROUP + STRONG_ITEMS,), jnp.int32)
    w_items = pltpu.SMEM((wp * count // GROUP + GROUP + WEAK_ITEMS,), jnp.int32)
    sem = pltpu.SemaphoreType.DMA
    pool_sems = nc + nr + cap + 4 * cap
    sent_sems = cap * (nc + nr) + 2

    def far(nb):
        own = sp + col * cap
        own_row = sp + (nc + row) * cap
        mine = (nb < sp) | ((nb >= own) & (nb < own + cap)) | ((nb >= own_row) & (nb < own_row + cap))
        return ~mine

    s_order, s_near = ordered(strong_nb, far(strong_nb), strong_live)
    w_order, w_near = ordered(weak_nb, far(weak_nb), jnp.full((wp,), count, jnp.int32))

    def exchange(col_out, row_out):
        got = lax.all_to_all(col_out, "col", split_axis=0, concat_axis=0, tiled=True)
        return got, [lax.ppermute(x, "row", perm(k + 1, nr)) for k, x in enumerate(row_out)]

    tiles, col_out, *row_out = call(
        prep_kernel,
        [(s_shape, BF16), col_shape] + row_shapes,
        [SM, HB, HB, HB],
        0, strong_amp.size * 8,
        [
            s_f32, s_bf16, pltpu.SMEM(col_send.shape, jnp.int32),
            pltpu.SMEM(row_send.shape, jnp.int32), sem((sent_sems + 6,)),
        ],
    )(me, col_send, row_send, strong_amp)
    got, row_got = exchange(col_out, row_out)
    s_acc, w_acc, s_inv, w_inv = call(
        functools.partial(first_kernel, nc),
        [(s_shape, F32), (w_shape, F32)] * 2,
        [SM] * 8 + [HB] * 11,
        a_flops + (s_flops + w_flops) // 2, s_bytes + w_bytes,
        [
            pool, s_f32, s_bf16, s_bf16, pltpu.VMEM(strong_energy.shape, F32), w_f32, w_f32,
            blocks, pltpu.VMEM(weak_energy.shape, F32), s_all, w_all, s_sums, w_sums, s_f32, w_f32,
            s_items, w_items, sem((pool_sems + 12,)), sem((sp,)), sem((wp,)),
        ],
    )(
        me, s_order, s_near, strong_live, w_order, w_near, col_send, row_send,
        tiles, strong_rhs, strong_left, strong_right, strong_energy, weak_amp, weak_rhs,
        weak_blocks, weak_energy, strong_intersection, weak_intersection,
    )
    amp1, tiles1, col_out1, *row_out1 = call(
        strong_kernel,
        [(s_shape, F32), (s_shape, BF16), col_shape] + row_shapes,
        [SM] * 6 + [HB, ANY] + [HB] * 4 + [ANY] * (nr - 1),
        s_flops // 2, s_bytes,
        [
            pool, s_all, s_sums, s_f32, s_f32, s_bf16, s_items, sem((pool_sems + sent_sems + 3,)),
            sem((sp,)),
        ],
    )(
        me, s_order, s_near, strong_live, col_send, row_send, tiles, got, strong_intersection,
        s_acc, s_inv, strong_amp, *row_got,
    )
    got1, row_got1 = exchange(col_out1, row_out1)
    w_amp1, s_acc1, w_acc1 = call(
        functools.partial(middle_kernel, nc),
        [(w_shape, F32), (s_shape, F32), (w_shape, F32)],
        [SM] * 8 + [HB, ANY] + [HB] * 11 + [ANY] * (nr - 1),
        a_flops + s_flops // 2 + w_flops, s_bytes + w_bytes,
        [
            pool, pool, w_sums, w_f32, w_f32, w_f32, blocks, s_f32, s_bf16, s_bf16, s_all, w_all,
            s_sums, s_items, w_items, sem((2 * pool_sems + 12,)), sem((2, max(sp, wp))),
        ],
    )(
        me, s_order, s_near, strong_live, w_order, w_near, col_send, row_send,
        tiles, got, tiles1, w_acc, w_inv, weak_amp, weak_rhs, weak_blocks, strong_rhs, strong_left,
        strong_right, strong_intersection, weak_intersection, *row_got,
    )
    s_out, w_out = call(
        last_kernel,
        [(s_shape, F32), (w_shape, F32)],
        [SM] * 7 + [HB, ANY] + [HB] * 8 + [ANY] * (nr - 1),
        (s_flops + w_flops) // 2, s_bytes + w_bytes,
        [
            pool, s_all, w_all, s_sums, w_sums, s_f32, w_f32, s_f32, w_f32, s_items, w_items,
            sem((pool_sems + 10,)), sem((sp,)), sem((wp,)),
        ],
    )(
        me, s_order, s_near, strong_live, w_order, w_near, row_send, tiles1, got1,
        strong_intersection, weak_intersection, s_acc1, w_acc1, s_inv, w_inv, amp1, w_amp1,
        *row_got1,
    )
    return s_out, w_out


def solution(mesh):
    nr, nc = mesh.shape["row"], mesh.shape["col"]
    whole = ("row", "col")
    ranks = (3, 3, 3, 3, 2, 4, 2, 1, 2, 2, 3, 3, 3, 2, 4, 2)
    in_specs = tuple(P(whole, *(None,) * (r - 1)) for r in ranks)
    out_specs = (P(whole, None, None), P(whole, None, None))
    return jax.shard_map(
        functools.partial(on_device, nr, nc),
        mesh=mesh, in_specs=in_specs, out_specs=out_specs, check_vma=False,
    )
```

time: 178 us -> 146 us (0.82)
  the two profiles are of different devices: /device:TPU:0 before, /device:TPU:13 now
where the time goes in v1:
time: 146 us; the launch traced here: 145 us
  Pallas kernels  119 us (82%)
  starting transfers between devices  15.1 us (10%)
  other arithmetic  5.35 us (4%)
  local copies, waits for them, and re-layouts  4.98 us (3%)
    pallas_call x1, Pallas kernels, on_device(): call(functools.partial(middle_kernel, nc), [(w_shape, F32), (s_shape, F32...  40.1 us
    pallas_call x1, Pallas kernels, on_device(): call(last_kernel, [(s_shape, F32), (w_shape, F32)], [SM] * 7 + [HB, ANY]...  31.6 us
    pallas_call x1, Pallas kernels, on_device(): call(functools.partial(first_kernel, nc), [(s_shape, F32), (w_shape, F32)...  29.3 us
    pallas_call x1, Pallas kernels, on_device(): call(strong_kernel, [(s_shape, F32), (s_shape, BF16), col_shape] + row_sh...  14.3 us
    all_to_all x2, starting transfers between devices, exchange(): lax.all_to_all(col_out, 'col', split_axis=0, concat_axis=0, tiled=True)  9.46 us
    ppermute x6, starting transfers between devices, exchange(): lax.ppermute(x, 'row', perm(k + 1, nr))  5.63 us
    unnamed x18, local copies, waits for them, and re-layouts  4.31 us
    pallas_call x1, Pallas kernels, on_device(): call(prep_kernel, [(s_shape, BF16), col_shape] + row_shapes, [SM, HB, HB,...  3.22 us
  transfers between devices with their start and end apart: 8, of which 0 were waited for; matrix products, arithmetic and copies ran while one was open for 4% of the time, Pallas kernels for 48%

profile of v1, /device:TPU:13, one launch (start us, length us, event | category | flops | bytes accessed | tf_op | source)
XLA Modules:
  0.0 144.9 jit_solution(13688870329711231178)
XLA Ops:
  0.6 1.3 copy.41.row_send_h.row_send
  1.9 1.3 copy.35.col_send_h.col_send
  3.3 0.6 pad_add_fusion.me
  3.9 3.2 %shard_map.167 = (bf16[16,128,128]{2,1,0:T(8,128)(2,1)}, bf16[8,2,128,128]{3,2,1,0:T(8,128)(2,1)}, bf16[2,128,128]{2,1,0:T(8,128)(2,1)}, bf16[2,128,128]{2,1,0:T(8,128)(2,1)}, bf16[2,128,128]{2,1,0:T(8,128)(2,1)}) custom-call(s32[2]{0:T(128)} %pad_add_fusion.me, s32[8,2]{1,0:T(8,128)} %copy.35.col_send_h.col_send, s32[4,2]{1,0:T(4,128)} %copy.41.row_send_h.row_send, ...), custom_call_target="tpu_custom_call" | custom-call | bytes 2097152 | tf_op jit(solution)/shard_map/pallas_call | solution.py:467
  7.1 5.7 %all-to-all-start = ((bf16[8,2,128,128]{3,2,1,0:T(8,128)(2,1)}), bf16[8,2,128,128]{3,2,1,0:T(8,128)(2,1)S(1)}, u32[]{:S(2)}, u32[]{:S(2)}) async-start(bf16[8,2,128,128]{3,2,1,0:T(8,128)(2,1)} %get-tuple-element.21), calls=%async_computation | async-start | bytes 1048576 | tf_op jit(solution)/shard_map/all_to_all | solution.py:464
  12.8 1.2 collective-permute-start
  14.1 0.2 collective-permute-start.1
  14.3 1.4 collective-permute-start.2
  15.7 1.3 convert_reduce_fusion.2
  17.0 0.1 iota_add_fusion
  17.1 0.7 copy.40.w_order
  17.8 1.4 convert_reduce_fusion.3
  19.2 0.7 iota_add_fusion.1
  19.9 0.4 convert_reduce_fusion.1
  20.4 0.7 select_reduce_fusion.1.s_order
  21.1 29.3 %shard_map.168 = (f32[16,128,128]{2,1,0:T(8,128)}, f32[32,64,64]{2,1,0:T(8,128)}, f32[16,128,128]{2,1,0:T(8,128)}, f32[32,64,64]{2,1,0:T(8,128)}) custom-call(s32[2]{0:T(128)} %pad_add_fusion.me, s32[16,16]{1,0:T(8,128)} %select_reduce_fusion.1.s_order, s32[16]{0:T(128)} %get-tuple-element.40.s_near, s32[16]{0:T(128)} %live.7, s32[32,16]{1,0:T(8,128)} %copy.40.w_order, ...), custom_call_target="tpu_custom_call" | custom-call | flops 2013265920 | bytes 16777216 | tf_op jit(solution)/shard_map/pallas_call | solution.py:478
  50.5 0.0 collective-permute-done.rest_0_
  50.5 0.0 copy-start.2
  50.5 0.0 collective-permute-done.1.rest_1_
  50.5 0.0 copy-start.3
  50.5 0.0 collective-permute-done.2.rest_2_
  50.5 0.0 copy-start.4
  50.5 0.0 all-to-all-done.got
  50.5 0.0 copy-start
  50.5 0.6 copy-done.2
  51.1 0.0 copy-done.3
  51.1 0.0 copy-done.4
  51.1 0.2 copy-done
  51.4 14.3 %shard_map.169 = (f32[16,128,128]{2,1,0:T(8,128)}, bf16[16,128,128]{2,1,0:T(8,128)(2,1)}, bf16[8,2,128,128]{3,2,1,0:T(8,128)(2,1)}, bf16[2,128,128]{2,1,0:T(8,12...) custom-call(s32[2]{0:T(128)} %pad_add_fusion.me, s32[16,16]{1,0:T(8,128)} %select_reduce_fusion.1.s_order, ...), custom_call_target="tpu_custom_call" | custom-call | flops 1073741824 | bytes 8388608 | tf_op jit(solution)/shard_map/pallas_call | solution.py:493
  65.7 3.8 %all-to-all-start.1 = ((bf16[8,2,128,128]{3,2,1,0:T(8,128)(2,1)}), bf16[8,2,128,128]{3,2,1,0:T(8,128)(2,1)S(1)}, u32[]{:S(2)}, u32[]{:S(2)}) async-start(bf16[8,2,128,128]{3,2,1,0:T(8,128)(2,1)} %get-tuple-element.28), calls=%async_computation.1 | async-start | bytes 1048576 | tf_op jit(solution)/shard_map/all_to_all | solution.py:464
  69.5 1.1 collective-permute-start.3
  70.6 0.0 collective-permute-start.4
  70.6 1.6 %collective-permute-start.5 = (bf16[2,128,128]{2,1,0:T(8,128)(2,1)}, bf16[2,128,128]{2,1,0:T(8,128)(2,1)S(1)}, u32[]{:S(2)}, u32[]{:S(2)}) collective-permute-start(bf16[2,128,128]{2,1,0:T(8,128)(2,1)} %get-tuple-element.37), channel_id=1, source_target_pairs={{0,24},{8,16},{16,8},{24,0},{1,25},{9,17},{17,9},{25,1},{2,26},{10... | collective-permute-start | bytes 196616 | tf_op jit(solution)/shard_map/ppermute | solution.py:465
  72.2 40.1 %shard_map.170 = (f32[32,64,64]{2,1,0:T(8,128)}, f32[16,128,128]{2,1,0:T(8,128)}, f32[32,64,64]{2,1,0:T(8,128)}) custom-call(s32[2]{0:T(128)} %pad_add_fusion.me, s32[16,16]{1,0:T(8,128)} %select_reduce_fusion.1.s_order, s32[16]{0:T(128)} %get-tuple-element.40.s_near, s32[16]{0:T(128)} %live.7, s32[32,16]{1,0:T(8,128)} %copy.40.w_order, ...), custom_call_target="tpu_custom_call" | custom-call | flops 2818572288 | bytes 16777216 | tf_op jit(solution)/shard_map/pallas_call | solution.py:507
  112.3 0.0 collective-permute-done.3.rest_0_
  112.3 0.0 copy-start.5
  112.4 0.0 collective-permute-done.4.rest_1_
  112.4 0.0 copy-start.6
  112.4 0.0 collective-permute-done.5.rest_2_
  112.4 0.0 copy-start.7
  112.4 0.0 all-to-all-done.1.got
  112.4 0.0 copy-start.1
  112.4 0.6 copy-done.5
  113.0 0.0 copy-done.6
  113.0 0.0 copy-done.7
  113.0 0.2 copy-done.1
  113.2 31.6 %shard_map.171 = (f32[16,128,128]{2,1,0:T(8,128)}, f32[32,64,64]{2,1,0:T(8,128)}) custom-call(s32[2]{0:T(128)} %pad_add_fusion.me, s32[16,16]{1,0:T(8,128)} %select_reduce_fusion.1.s_order, s32[16]{0:T(128)} %get-tuple-element.40.s_near, s32[16]{0:T(128)} %live.7, s32[32,16]{1,0:T(8,128)} %copy.40.w_order, s32[32]{0:T(128)} %get-tuple-element.38.w_near, ...), custom_call_target="tpu_custom_call" | custom-call | flops 1879048192 | bytes 16777216 | tf_op jit(solution)/shard_map/pallas_call | solution.py:521
  (4 shorter events, 0.1 us)
Async XLA Ops:
  7.1 43.4 %all-to-all-start = ((bf16[8,2,128,128]{3,2,1,0:T(8,128)(2,1)}), bf16[8,2,128,128]{3,2,1,0:T(8,128)(2,1)S(1)}, u32[]{:S(2)}, u32[]{:S(2)}) async-start(bf16[8,2,128,128]{3,2,1,0:T(8,128)(2,1)} %get-tuple-element.21), calls=%async_computation | async-start | bytes 1048576 | tf_op jit(solution)/shard_map/all_to_all | solution.py:464
  12.8 37.6 %collective-permute-start = (bf16[2,128,128]{2,1,0:T(8,128)(2,1)}, bf16[2,128,128]{2,1,0:T(8,128)(2,1)S(1)}, u32[]{:S(2)}, u32[]{:S(2)}) collective-permute-start(bf16[2,128,128]{2,1,0:T(8,128)(2,1)} %get-tuple-element.24), channel_id=1, source_target_pairs={{0,8},{8,0},{16,24},{24,16},{1,9},{9,1},{17,25},{25,17},{2,10},{10... | collective-permute-start | bytes 196616 | tf_op jit(solution)/shard_map/ppermute | solution.py:465
  14.1 36.4 %collective-permute-start.1 = (bf16[2,128,128]{2,1,0:T(8,128)(2,1)}, bf16[2,128,128]{2,1,0:T(8,128)(2,1)S(1)}, u32[]{:S(2)}, u32[]{:S(2)}) collective-permute-start(bf16[2,128,128]{2,1,0:T(8,128)(2,1)} %get-tuple-element.25), channel_id=1, source_target_pairs={{0,16},{8,24},{16,0},{24,8},{1,17},{9,25},{17,1},{25,9},{2,18},{10... | collective-permute-start | bytes 196616 | tf_op jit(solution)/shard_map/ppermute | solution.py:465
  14.3 36.2 %collective-permute-start.2 = (bf16[2,128,128]{2,1,0:T(8,128)(2,1)}, bf16[2,128,128]{2,1,0:T(8,128)(2,1)S(1)}, u32[]{:S(2)}, u32[]{:S(2)}) collective-permute-start(bf16[2,128,128]{2,1,0:T(8,128)(2,1)} %get-tuple-element.26), channel_id=1, source_target_pairs={{0,24},{8,16},{16,8},{24,0},{1,25},{9,17},{17,9},{25,1},{2,26},{10... | collective-permute-start | bytes 196616 | tf_op jit(solution)/shard_map/ppermute | solution.py:465
  50.5 0.6 copy-start.2
  50.5 0.6 copy-start.3
  50.5 0.6 copy-start.4
  50.5 0.8 copy-start
  65.7 46.7 %all-to-all-start.1 = ((bf16[8,2,128,128]{3,2,1,0:T(8,128)(2,1)}), bf16[8,2,128,128]{3,2,1,0:T(8,128)(2,1)S(1)}, u32[]{:S(2)}, u32[]{:S(2)}) async-start(bf16[8,2,128,128]{3,2,1,0:T(8,128)(2,1)} %get-tuple-element.28), calls=%async_computation.1 | async-start | bytes 1048576 | tf_op jit(solution)/shard_map/all_to_all | solution.py:464
  69.5 42.9 %collective-permute-start.3 = (bf16[2,128,128]{2,1,0:T(8,128)(2,1)}, bf16[2,128,128]{2,1,0:T(8,128)(2,1)S(1)}, u32[]{:S(2)}, u32[]{:S(2)}) collective-permute-start(bf16[2,128,128]{2,1,0:T(8,128)(2,1)} %get-tuple-element.35), channel_id=1, source_target_pairs={{0,8},{8,0},{16,24},{24,16},{1,9},{9,1},{17,25},{25,17},{2,10},{10... | collective-permute-start | bytes 196616 | tf_op jit(solution)/shard_map/ppermute | solution.py:465
  70.6 41.8 %collective-permute-start.4 = (bf16[2,128,128]{2,1,0:T(8,128)(2,1)}, bf16[2,128,128]{2,1,0:T(8,128)(2,1)S(1)}, u32[]{:S(2)}, u32[]{:S(2)}) collective-permute-start(bf16[2,128,128]{2,1,0:T(8,128)(2,1)} %get-tuple-element.36), channel_id=1, source_target_pairs={{0,16},{8,24},{16,0},{24,8},{1,17},{9,25},{17,1},{25,9},{2,18},{10... | collective-permute-start | bytes 196616 | tf_op jit(solution)/shard_map/ppermute | solution.py:465
  70.6 41.8 %collective-permute-start.5 = (bf16[2,128,128]{2,1,0:T(8,128)(2,1)}, bf16[2,128,128]{2,1,0:T(8,128)(2,1)S(1)}, u32[]{:S(2)}, u32[]{:S(2)}) collective-permute-start(bf16[2,128,128]{2,1,0:T(8,128)(2,1)} %get-tuple-element.37), channel_id=1, source_target_pairs={{0,24},{8,16},{16,8},{24,0},{1,25},{9,17},{17,9},{25,1},{2,26},{10... | collective-permute-start | bytes 196616 | tf_op jit(solution)/shard_map/ppermute | solution.py:465
  112.3 0.6 copy-start.5
  112.4 0.6 copy-start.6
  112.4 0.6 copy-start.7
  112.4 0.8 copy-start.1
